TPU v7x, 32 devices: a whole 2x2x4 slice. The times are simulated.
32 devices in a mesh: energy: 4 (over z), wire: 8 (over y, x, core).
Axes of the slice: x: 2, y: 2, z: 4, core: 2. Of those that a mesh axis runs over, the one named last changes fastest.
Arguments:
- g_prev: bfloat16 [2, 8, 8, 512, 512], P(None, 'energy', 'wire'), may hold values from -0.25 to 0.25
- local_green: bfloat16 [2, 8, 8, 512, 512], P(None, 'energy', 'wire'), may hold values from -0.09375 to 0.09375
- prop: bfloat16 [2, 8, 8, 512, 512], P(None, 'energy', 'wire'), may hold values from -1.5 to 1.5
- incoming: bfloat16 [2, 8, 8, 64, 512], P(None, 'energy', 'wire'), may hold values from -3 to 3
- plus_partner: int32 [8], replicated, may hold values from -1 to 7
- minus_partner: int32 [8], replicated, may hold values from -1 to 7
- counts: int32 [4], P('energy'), may hold values from 1 to 2
- pot_index: int32 [8], P('wire'), may hold values from 0 to 15
- levels: float32 [16], replicated, may hold values from -1 to 1
- coupling: float32 [2], replicated, may hold values from 0.5 to 2
Outputs:
- scattered: bfloat16 [2, 8, 8, 64, 512], P(None, 'energy', 'wire')
- green_next: bfloat16 [2, 8, 8, 512, 512], P(None, 'energy', 'wire')
Inputs may be any that keep to these rules, and one draw needn't show every extreme that they name: `plus_partner`: -1 means that the partner energy lies outside the window. `minus_partner`: -1 means that the partner energy lies outside the window. The first counts[g] of the 2 slots of group g are live.
All inputs are finite; a program needn't handle non-finite values.
Results may differ from a plain program's by a relative error of at most 0.035.
Values may be sent and summed in bfloat16 or wider, within the bound.
No kernel may reach another device: no remote copies, remote signals or barrier semaphores. Data moves between devices by JAX's collectives and lax.ppermute only.
A program may use at most 192 MiB of HBM per device.

v0:
```python
import jax
import jax.numpy as jnp
from jax import lax
from jax.sharding import PartitionSpec as P


def entering(value, axis, join, neutral):
    count, mine = (lax.axis_size(axis), lax.axis_index(axis))
    pieces = jax.tree.map(lambda part: lax.all_gather(part, axis), value)
    subtotal = jax.tree.map(
        lambda part, zero: jnp.full_like(part, 0) + jnp.asarray(zero, part.dtype), value, neutral
    )

    def step(position, subtotal):
        longer = join(subtotal, jax.tree.map(lambda part: part[position], pieces))
        return jax.tree.map(lambda new, old: jnp.where(position < mine, new, old), longer, subtotal)

    return lax.fori_loop(0, count - 1, step, subtotal)


def complex_product(first_op, second_op):

    def multiply(lhs_part, rhs_part):
        return jnp.einsum("sij,sjk->sik", lhs_part, rhs_part, preferred_element_type=jnp.float32)

    real_part = multiply(first_op[0], second_op[0]) - multiply(first_op[1], second_op[1])
    imag_part = multiply(first_op[0], second_op[1]) + multiply(first_op[1], second_op[0])
    return jnp.stack([real_part, imag_part])


def intersection(first_op, second_op):
    return jnp.einsum("smi,smj->sij", first_op, second_op, preferred_element_type=jnp.float32)


def shards(
    g_prev,
    local_green,
    prop,
    incoming,
    plus_partner,
    minus_partner,
    counts,
    pot_index,
    levels,
    coupling,
):
    slot_count = g_prev.shape[1]
    orbitals = g_prev.shape[3]
    mode_count = incoming.shape[3]
    group_index = lax.axis_index("energy")
    plus_own = lax.dynamic_slice_in_dim(plus_partner, group_index * slot_count, slot_count)
    minus_own = lax.dynamic_slice_in_dim(minus_partner, group_index * slot_count, slot_count)
    incident = incoming[:, :, 0]
    green_here = local_green[:, :, 0]
    steps_here = prop[:, :, 0]
    shard_piece = lax.all_gather(g_prev, "energy", axis=1, tiled=True)
    global_index = jnp.arange(shard_piece.shape[1], dtype=jnp.int32)
    slab_piece = shard_piece[:, :, 0]
    plus_select = (plus_own[:, None] == global_index[None, :]).astype(jnp.bfloat16)
    minus_select = (minus_own[:, None] == global_index[None, :]).astype(jnp.bfloat16)

    def select_rows(selector):
        return jnp.einsum(
            "sk,rkab->rsab", selector, slab_piece, preferred_element_type=jnp.float32
        ).astype(jnp.bfloat16)

    upper_block = select_rows(plus_select)
    lower_block = select_rows(minus_select)
    shifted = coupling[0] * complex_product(incident, upper_block) + coupling[1] * complex_product(
        incident, lower_block
    )
    level_hit = pot_index[0] == jnp.arange(levels.shape[0], dtype=jnp.int32)
    potential = jnp.sum(jnp.where(level_hit, levels, jnp.float32(0.0)))
    source_term = (shifted + potential * incident.astype(jnp.float32)).astype(jnp.bfloat16)
    source = complex_product(source_term, green_here)
    identity = jnp.broadcast_to(
        jnp.eye(orbitals, dtype=jnp.bfloat16), (slot_count, orbitals, orbitals)
    )
    identity_map = jnp.stack([identity, jnp.zeros_like(identity)])
    zero_wave = jnp.zeros((2, slot_count, mode_count, orbitals), jnp.bfloat16)

    def compose(earlier, later):
        step_block = complex_product(earlier[0], later[0]).astype(jnp.bfloat16)
        offset_wave = (complex_product(earlier[1], later[0]) + later[1].astype(jnp.float32)).astype(
            jnp.bfloat16
        )
        return (step_block, offset_wave)

    preceding = entering(
        (steps_here, source.astype(jnp.bfloat16)), "wire", compose, (identity_map, zero_wave)
    )
    chained = (complex_product(preceding[1], steps_here) + source).astype(jnp.bfloat16)
    combined = (incident.astype(jnp.float32) + chained.astype(jnp.float32)).astype(jnp.bfloat16)
    green_real = (
        intersection(combined[1], combined[0]) - intersection(combined[0], combined[1])
    ) / mode_count
    green_imag = (
        intersection(combined[0], combined[0]) + intersection(combined[1], combined[1])
    ) / mode_count
    live_mask = (jnp.arange(slot_count, dtype=jnp.int32) < counts[0])[None, :, None, None]
    scattered = jnp.where(live_mask, chained, jnp.zeros_like(chained))[:, :, None]
    green_block = jnp.stack([green_real, green_imag])
    green_next = jnp.where(live_mask, green_block, jnp.zeros_like(green_block)).astype(
        jnp.bfloat16
    )[:, :, None]
    return (scattered, green_next)


def solution(mesh):
    placed = (
        P(None, "energy", "wire", None, None),
        P(None, "energy", "wire", None, None),
        P(None, "energy", "wire", None, None),
        P(None, "energy", "wire", None, None),
        P(),
        P(),
        P("energy"),
        P("wire"),
        P(),
        P(),
    )
    return jax.shard_map(
        shards,
        mesh=mesh,
        in_specs=placed,
        out_specs=(P(None, "energy", "wire", None, None), P(None, "energy", "wire", None, None)),
        check_vma=False,
    )
```

profile of v0, /device:TPU:0, one launch (start us, length us, event | category | flops | bytes accessed | tf_op | source)
XLA Modules:
  0.0 369.7 jit_solution(1472527370898223248)
XLA Ops:
  7.2 3.0 copy.30
  13.0 149.8 %all-gather.5.cloned.1.call-done = bf16[2,8,1,512,512]{4,3,2,0,1:T(8,128)(2,1)} async-done(((bf16[2,2,1,512,512]{4,3,2,0,1:T(8,128)(2,1)}), bf16[2,8,1,512,512]{4,3,2,0,1:T(8,128)(2,1)}) %all-gather.5.cloned.1.call-update) | async-done | bytes 8388624 | tf_op jit(solution)/shard_map/all_gather | solution.py:56
  162.8 9.0 %fusion.23 = bf16[2,2,512,512]{3,1,2,0:T(2,128)(2,1)S(1)} fusion(bf16[2,8,1,512,512]{4,3,2,0,1:T(8,128)(2,1)} %all-gather.5.cloned.1.call-done, s32[2]{0:T(128)S(1)} %dynamic_slice.21), kind=kOutput, calls=%fused_computation.28 | convolution fusion | flops 17825808 | bytes 10485768 | tf_op jit(solution)/shard_map/sk,rkab->rsab/dot_general | solution.py:63
  171.8 1.7 slice_bitcast_fusion.11
  174.8 5.2 %fusion.26 = bf16[2,2,512,512]{3,1,2,0:T(2,128)(2,1)S(1)} fusion(bf16[2,8,1,512,512]{4,3,2,0,1:T(8,128)(2,1)S(1)} %bitcast.196, s32[2]{0:T(128)S(1)} %dynamic_slice.20), kind=kOutput, calls=%fused_computation.29 | convolution fusion | flops 17825808 | bytes 10485768 | tf_op jit(solution)/shard_map/sk,rkab->rsab/dot_general | solution.py:63
  182.7 2.1 fusion.51
  189.3 24.9 %all-gather.7.cloned.1.call-done = bf16[8,2,2,64,512]{4,3,2,1,0:T(8,128)(2,1)} async-done(((bf16[1,2,2,64,512]{4,3,2,1,0:T(8,128)(2,1)}), bf16[8,2,2,64,512]{4,3,2,1,0:T(8,128)(2,1)}) %all-gather.7.cloned.1.call-update) | async-done | bytes 2097168 | tf_op jit(solution)/shard_map/all_gather | solution.py:9
  214.2 91.8 %all-gather.9.cloned.1.call-done = bf16[16,2,1,512,512]{4,3,2,1,0:T(8,128)(2,1)} async-done(((bf16[2,2,1,512,512]{4,3,2,1,0:T(8,128)(2,1)}), bf16[16,2,1,512,512]{4,3,2,1,0:T(8,128)(2,1)}) %all-gather.9.cloned.1.call-update) | async-done | bytes 16777232 | tf_op jit(solution)/shard_map/all_gather | solution.py:9
  306.0 51.0 %while.14 = (s32[]{:T(128)}, bf16[2,2,64,512]{3,2,1,0:T(8,128)(2,1)S(1)}, s32[]{:T(128)}, bf16[8,2,2,512,512]{4,3,2,1,0:T(8,128)(2,1)}, bf16[8,2,2,64,512]{4,3,2,1,0:T(8,128)(2,1)}, /*index=5*/s32[]{:T(128)}, s32[]{:T(128)}, s32[]{}) while((s32[]{:T(128)}, bf16[2,2,64,512]{3,2,1,0:T(8,128)(2,1)S(1)}, s32[]{:T(128)}, ...), condition=%wide.region_2.3_spmd.clone, body=%wide.region_1.2_spmd.clone.sunk | while | flops 269484032 | bytes 8128642 | solution.py:18
  306.0 1.7 fusion.85
  307.7 1.5 fusion.86
  309.2 1.5 fusion.83
  310.7 1.5 fusion.84
  313.4 1.5 fusion.85
  314.9 1.5 fusion.86
  316.5 1.5 fusion.83
  318.0 1.5 fusion.84
  322.2 1.5 fusion.86
  323.7 1.5 fusion.83
  325.2 1.5 fusion.84
  329.5 1.5 fusion.86
  331.0 1.5 fusion.83
  332.5 1.5 fusion.84
  336.7 1.5 fusion.86
  338.2 1.5 fusion.83
  339.8 1.5 fusion.84
  344.0 1.5 fusion.86
  345.5 1.5 fusion.83
  347.0 1.5 fusion.84
  351.2 1.5 fusion.86
  354.3 1.5 fusion.84
  360.4 2.0 fusion.29
  (84 shorter events, 30.9 us)
Async XLA Ops:
  7.2 155.6 %all-gather.5.cloned.1.call-start = ((), (), s32[]{:S(2)}) async-start(), calls=%async_computation | async-start | bytes 10485760 | tf_op jit(solution)/shard_map/all_gather | solution.py:56
  10.3 0.7 copy-start.8
  10.3 0.7 copy-start.9
  10.3 1.5 copy-start.7
  10.3 2.1 copy-start.10
  10.3 203.9 %all-gather.7.cloned.1.call-start = ((), (), s32[]{:S(2)}) async-start(), calls=%async_computation.1 | async-start | bytes 2359296 | tf_op jit(solution)/shard_map/all_gather | solution.py:9
  162.8 10.7 %copy-start.1 = (bf16[2,2,1,64,512]{4,3,2,1,0:T(8,128)(2,1)S(1)}, bf16[2,2,1,64,512]{4,3,2,1,0:T(8,128)(2,1)}, u32[]{:S(2)}) copy-start(bf16[2,2,1,64,512]{4,3,2,1,0:T(8,128)(2,1)} %param.15) | copy-start | bytes 786436
  162.8 12.0 %slice-start = ((s8[8388608]{0:T(1024)(128)(4,1)}), s8[4194304]{0:T(1024)(128)(4,1)S(1)}, s32[]{:S(2)}) async-start(s8[8388608]{0:T(1024)(128)(4,1)} %bitcast.195), calls=%async_computation.3 | async-start | bytes 8388608
  171.8 2.9 slice-start.1
  182.1 2.8 copy-start.2
  185.7 0.7 copy-start.3
  186.4 0.7 copy-start.5
  187.9 118.1 %all-gather.9.cloned.1.call-start = ((), (), s32[]{:S(2)}) async-start(), calls=%async_computation.2 | async-start | bytes 18874368 | tf_op jit(solution)/shard_map/all_gather | solution.py:9
  306.0 51.0 %copy-start = (bf16[2,2,1,512,512]{4,3,2,1,0:T(8,128)(2,1)S(1)}, bf16[2,2,1,512,512]{4,3,2,1,0:T(8,128)(2,1)}, u32[]{:S(2)}) copy-start(bf16[2,2,1,512,512]{4,3,2,1,0:T(8,128)(2,1)} %param.14) | copy-start | bytes 6291460
  357.2 1.0 copy-start.4
  357.3 1.0 copy-start.6
Sparse Core Ops, SparseCore 0:
  10.4 152.3 all-gather.4
  188.0 26.1 all-gather.6
  216.1 89.8 all-gather.8
where the time goes:
time: 371 us; the launch traced here: 370 us
  waiting for transfers between devices  267 us (72%)
  matrix products  63.7 us (17%)
  between operations  15.3 us (4%)
  other arithmetic  14.3 us (4%)
  local copies, waits for them, and re-layouts  8.73 us (2%)
    all_gather x1, waiting for transfers between devices, shards(): shard_piece = lax.all_gather(g_prev, 'energy', axis=1, tiled=True)  150 us
    all_gather x2, waiting for transfers between devices, entering(): pieces = jax.tree.map(lambda part: lax.all_gather(part, axis), value)  117 us
    dot_general x44, matrix products, multiply(): jnp.einsum('sij,sjk->sik', lhs_part, rhs_part, preferred_element_type=jnp...  47.6 us
    dot_general x2, matrix products, select_rows(): jnp.einsum('sk,rkab->rsab', selector, slab_piece, preferred_element_type=...  14.2 us
    select_n x7, other arithmetic, step(): jnp.where(position < mine, new, old)  7.62 us
  transfers between devices with their start and end apart: 3, of which 3 were waited for; matrix products, arithmetic and copies ran while one was open for 0% of the time, Pallas kernels for 0%

commit v1 on v0

--- a/solution.py
+++ b/solution.py
@@ -2,6 +2,34 @@
 import jax.numpy as jnp
 from jax import lax
 from jax.sharding import PartitionSpec as P
+
+
+def try_all_side_on(u_in, link_axis, on_dim):
+    b_next = jax.lax.axis_index(link_axis)
+    outer = jax.lax.axis_size(link_axis)
+    newest, after, row_out = (outer, b_next, u_in.shape[on_dim])
+    g_now = range(newest)
+    made = list(map(lambda b: (b, (b + 1) % newest), range(newest)))
+    views = list(map(lambda b: (b, (b - 1) % newest), g_now))
+    then = jnp.zeros(
+        (*u_in.shape[:on_dim], newest * row_out, *u_in.shape[on_dim + 1 :]), u_in.dtype
+    )
+    tmp = y_new = u_in
+    e_now = newest // 2
+    s = 1
+    then = lax.dynamic_update_slice_in_dim(then, u_in, after * row_out, axis=on_dim)
+    while s < e_now + 1:
+        tmp = jax.lax.ppermute(tmp, link_axis, made)
+        then = lax.dynamic_update_slice_in_dim(
+            then, tmp, (after - s) % newest * row_out, axis=on_dim
+        )
+        if s < newest - e_now:
+            y_new = jax.lax.ppermute(y_new, axis_name=link_axis, perm=views)
+            then = lax.dynamic_update_slice_in_dim(
+                then, y_new, (after + s) % newest * row_out, axis=on_dim
+            )
+        s += 1
+    return then
 
 
 def entering(value, axis, join, neutral):
@@ -53,7 +81,7 @@
     incident = incoming[:, :, 0]
     green_here = local_green[:, :, 0]
     steps_here = prop[:, :, 0]
-    shard_piece = lax.all_gather(g_prev, "energy", axis=1, tiled=True)
+    shard_piece = try_all_side_on(g_prev, "energy", 1)
     global_index = jnp.arange(shard_piece.shape[1], dtype=jnp.int32)
     slab_piece = shard_piece[:, :, 0]
     plus_select = (plus_own[:, None] == global_index[None, :]).astype(jnp.bfloat16)

time: 371 us -> 354 us (0.954)
  waiting for transfers between devices: 267 us -> 235 us
  local copies, waits for them, and re-layouts: 8.73 us -> 26.7 us
  matrix products: 63.7 us -> 54.3 us
  starting transfers between devices: 0.12 us -> 5.25 us
    all_gather x1 -> x0, waiting for transfers between devices: 150 us -> none  [shards(): shard_piece = lax.all_gather(g_prev, 'energy', axis=1, tiled=True)]
    ppermute x0 -> x3, waiting for transfers between devices: none -> 117 us  [the longest x2 86.8 us: try_all_side_on(): tmp = jax.lax.ppermute(tmp, link_axis, made)]
    dynamic_update_slice x0 -> x4, local copies, waits for them, and re-layouts: none -> 17.8 us  [the longest x2 8.83 us: try_all_side_on(): lax.dynamic_update_slice_in_dim(then, tmp, (after - s) % newest * row_out...]
    dot_general x2, matrix products: 14.2 us -> 4.77 us  [select_rows(): jnp.einsum('sk,rkab->rsab', selector, slab_piece, preferred_element_type=...]
    ppermute x0 -> x3, starting transfers between devices: none -> 5.17 us  [the longest x2 3.08 us: try_all_side_on(): tmp = jax.lax.ppermute(tmp, link_axis, made)]
  transfers between devices with their start and end apart: 3 -> 5, of which waited for: 3 -> 5; matrix products, arithmetic and copies ran while one was open for 0% -> 5% of each run, Pallas kernels for 0% -> 0%
where the time goes in v1:
time: 354 us; the launch traced here: 352 us
  waiting for transfers between devices  235 us (66%)
  matrix products  54.3 us (15%)
  local copies, waits for them, and re-layouts  26.7 us (8%)
  between operations  15.6 us (4%)
  other arithmetic  14.8 us (4%)
  starting transfers between devices  5.25 us (1%)
    all_gather x2, waiting for transfers between devices, entering(): pieces = jax.tree.map(lambda part: lax.all_gather(part, axis), value)  118 us
    ppermute x2, waiting for transfers between devices, try_all_side_on(): tmp = jax.lax.ppermute(tmp, link_axis, made)  86.8 us
    dot_general x44, matrix products, multiply(): jnp.einsum('sij,sjk->sik', lhs_part, rhs_part, preferred_element_type=jnp...  47.6 us
    ppermute x1, waiting for transfers between devices, try_all_side_on(): y_new = jax.lax.ppermute(y_new, axis_name=link_axis, perm=views)  30 us
    dynamic_update_slice x2, local copies, waits for them, and re-layouts, try_all_side_on(): lax.dynamic_update_slice_in_dim(then, tmp, (after - s) % newest * row_out...  8.83 us
    select_n x7, other arithmetic, step(): jnp.where(position < mine, new, old)  7.62 us
  transfers between devices with their start and end apart: 5, of which 5 were waited for; matrix products, arithmetic and copies ran while one was open for 5% of the time, Pallas kernels for 0%

profile of v1, /device:TPU:0, one launch (start us, length us, event | category | flops | bytes accessed | tf_op | source)
XLA Modules:
  0.0 352.2 jit_solution(13773061640856514690)
XLA Ops:
  7.2 3.1 collective-permute-start
  10.3 2.1 collective-permute-start.1
  12.4 46.6 %collective-permute-done = bf16[2,2,1,512,512]{4,3,2,1,0:T(8,128)(2,1)S(1)} collective-permute-done((bf16[2,2,1,512,512]{4,3,2,1,0:T(8,128)(2,1)}, bf16[2,2,1,512,512]{4,3,2,1,0:T(8,128)(2,1)S(1)}, u32[]{:S(2)}, u32[]{:S(2)}) %collective-permute-start) | collective-permute-done | bytes 2097184 | tf_op jit(solution)/shard_map/ppermute | solution.py:22
  65.4 3.8 %copy_dynamic-update-slice_fusion.3 = bf16[2,8,512,512]{3,1,2,0:T(8,128)(2,1)S(1)} fusion(bf16[2,8,512,512]{3,1,2,0:T(8,128)(2,1)S(1)} %squeeze.140, s32[]{:T(128)S(6)} %select_n.77, bf16[2,2,512,512]{3,2,1,0:T(8,128)(2,1)S(1)} %bitcast.213), kind=kLoop, calls=%fused_computation.28 | loop fusion | bytes 4194308 | tf_op jit(solution)/shard_map/dynamic_update_slice | solution.py:20
  69.2 3.6 %copy_dynamic-update-slice_fusion.2 = bf16[2,8,512,512]{3,1,2,0:T(8,128)(2,1)S(1)} fusion(bf16[2,8,512,512]{3,1,2,0:T(8,128)(2,1)S(1)} %copy_dynamic-update-slice_fusion.3, s32[]{:T(128)S(6)} %select_n.79, bf16[2,2,512,512]{3,2,1,0:T(8,128)(2,1)S(1)} %bitcast.214), kind=kLoop, calls=%fused_computation.27 | loop fusion | bytes 4194308 | tf_op jit(solution)/shard_map/dynamic_update_slice | solution.py:23
  72.8 30.0 %collective-permute-done.1 = bf16[2,2,1,512,512]{4,3,2,1,0:T(8,128)(2,1)} collective-permute-done((bf16[2,2,1,512,512]{4,3,2,1,0:T(8,128)(2,1)}, bf16[2,2,1,512,512]{4,3,2,1,0:T(8,128)(2,1)}, u32[]{:S(2)}, u32[]{:S(2)}) %collective-permute-start.1) | collective-permute-done | bytes 2097184 | tf_op jit(solution)/shard_map/ppermute | solution.py:27
  102.8 5.2 %copy_dynamic-update-slice_fusion.1 = bf16[2,8,512,512]{3,1,2,0:T(8,128)(2,1)S(1)} fusion(bf16[2,8,512,512]{3,1,2,0:T(8,128)(2,1)S(1)} %copy_dynamic-update-slice_fusion.2, s32[]{:T(128)S(6)} %select_n.81, bf16[2,2,512,512]{3,2,1,0:T(8,128)(2,1)} %bitcast.5), kind=kLoop, calls=%fused_computation.26 | loop fusion | bytes 4194308 | tf_op jit(solution)/shard_map/dynamic_update_slice | solution.py:28
  108.1 40.1 %collective-permute-done.2 = bf16[2,2,1,512,512]{4,3,2,1,0:T(8,128)(2,1)} collective-permute-done((bf16[2,2,1,512,512]{4,3,2,1,0:T(8,128)(2,1)S(1)}, bf16[2,2,1,512,512]{4,3,2,1,0:T(8,128)(2,1)}, u32[]{:S(2)}, u32[]{:S(2)}) %collective-permute-start.2) | collective-permute-done | bytes 2097184 | tf_op jit(solution)/shard_map/ppermute | solution.py:22
  148.2 5.2 %copy_dynamic-update-slice_fusion = bf16[2,8,512,512]{3,1,2,0:T(8,128)(2,1)S(1)} fusion(bf16[2,8,512,512]{3,1,2,0:T(8,128)(2,1)S(1)} %copy_dynamic-update-slice_fusion.1, s32[]{:T(128)S(6)} %select_n.83, bf16[2,2,512,512]{3,2,1,0:T(8,128)(2,1)} %bitcast.6), kind=kLoop, calls=%fused_computation.25 | loop fusion | bytes 4194308 | tf_op jit(solution)/shard_map/dynamic_update_slice | solution.py:23
  153.4 2.4 fusion.12
  155.8 1.7 slice_bitcast_fusion.11
  158.8 2.4 fusion.11
  163.9 2.1 fusion.35
  170.5 26.0 %all-gather.4.cloned.1.call-done = bf16[8,2,2,64,512]{4,3,2,1,0:T(8,128)(2,1)} async-done(((bf16[1,2,2,64,512]{4,3,2,1,0:T(8,128)(2,1)}), bf16[8,2,2,64,512]{4,3,2,1,0:T(8,128)(2,1)}) %all-gather.4.cloned.1.call-update) | async-done | bytes 2097168 | tf_op jit(solution)/shard_map/all_gather | solution.py:37
  196.4 91.8 %all-gather.6.cloned.1.call-done = bf16[16,2,1,512,512]{4,3,2,1,0:T(8,128)(2,1)} async-done(((bf16[2,2,1,512,512]{4,3,2,1,0:T(8,128)(2,1)}), bf16[16,2,1,512,512]{4,3,2,1,0:T(8,128)(2,1)}) %all-gather.6.cloned.1.call-update) | async-done | bytes 16777232 | tf_op jit(solution)/shard_map/all_gather | solution.py:37
  288.2 51.0 %while.14 = (s32[]{:T(128)}, bf16[2,2,64,512]{3,2,1,0:T(8,128)(2,1)S(1)}, s32[]{:T(128)}, bf16[8,2,2,512,512]{4,3,2,1,0:T(8,128)(2,1)}, bf16[8,2,2,64,512]{4,3,2,1,0:T(8,128)(2,1)}, /*index=5*/s32[]{:T(128)}, s32[]{:T(128)}, s32[]{}) while((s32[]{:T(128)}, bf16[2,2,64,512]{3,2,1,0:T(8,128)(2,1)S(1)}, s32[]{:T(128)}, ...), condition=%wide.region_2.3_spmd.clone, body=%wide.region_1.2_spmd.clone.sunk | while | flops 269484032 | bytes 8128642 | solution.py:46
  288.2 1.7 fusion.71
  289.9 1.5 fusion.72
  291.4 1.5 fusion.69
  293.0 1.5 fusion.70
  297.2 1.5 fusion.72
  298.7 1.5 fusion.69
  304.4 1.5 fusion.72
  306.0 1.5 fusion.69
  311.7 1.5 fusion.72
  314.8 1.5 fusion.70
  319.0 1.5 fusion.72
  320.5 1.5 fusion.69
  326.2 1.5 fusion.72
  329.3 1.5 fusion.70
  333.5 1.5 fusion.72
  342.6 2.0 fusion.13
  (80 shorter events, 45.2 us)
Async XLA Ops:
  7.2 189.3 %all-gather.4.cloned.1.call-start = ((), (), s32[]{:S(2)}) async-start(), calls=%async_computation | async-start | bytes 2359296 | tf_op jit(solution)/shard_map/all_gather | solution.py:37
  7.2 51.8 %collective-permute-start = (bf16[2,2,1,512,512]{4,3,2,1,0:T(8,128)(2,1)}, bf16[2,2,1,512,512]{4,3,2,1,0:T(8,128)(2,1)S(1)}, u32[]{:S(2)}, u32[]{:S(2)}) collective-permute-start(bf16[2,2,1,512,512]{4,3,2,1,0:T(8,128)(2,1)} %param.12), channel_id=1, source_target_pairs={{0,8},{8,16},{16,24},{24,0},{1,9},{9,17},{17,25},{25,1},{2,10},{10... | collective-permute-start | bytes 6291464 | tf_op jit(solution)/shard_map/ppermute | solution.py:22
  10.3 92.6 %collective-permute-start.1 = (bf16[2,2,1,512,512]{4,3,2,1,0:T(8,128)(2,1)}, bf16[2,2,1,512,512]{4,3,2,1,0:T(8,128)(2,1)}, u32[]{:S(2)}, u32[]{:S(2)}) collective-permute-start(bf16[2,2,1,512,512]{4,3,2,1,0:T(8,128)(2,1)} %param.12), channel_id=1, source_target_pairs={{0,24},{8,0},{16,8},{24,16},{1,25},{9,1},{17,9},{25,17},{2,26},{10... | collective-permute-start | bytes 6291464 | tf_op jit(solution)/shard_map/ppermute | solution.py:27
  59.0 89.2 %collective-permute-start.2 = (bf16[2,2,1,512,512]{4,3,2,1,0:T(8,128)(2,1)S(1)}, bf16[2,2,1,512,512]{4,3,2,1,0:T(8,128)(2,1)}, u32[]{:S(2)}, u32[]{:S(2)}) collective-permute-start(bf16[2,2,1,512,512]{4,3,2,1,0:T(8,128)(2,1)S(1)} %collective-permute-done), channel_id=1, source_target_pairs={{0,8},{8,16},{16,24},{24,0},{1,9},{9,17},{17,25},{25,1},{2,10},{10... | collective-permute-start | bytes 6291464 | tf_op jit(solution)/shard_map/ppermute | solution.py:22
  63.8 1.6 copy-start.7
  155.8 1.7 copy-start.1
  163.2 2.7 copy-start.2
  166.9 0.7 copy-start.3
  167.6 0.7 copy-start.5
  169.0 119.2 %all-gather.6.cloned.1.call-start = ((), (), s32[]{:S(2)}) async-start(), calls=%async_computation.1 | async-start | bytes 18874368 | tf_op jit(solution)/shard_map/all_gather | solution.py:37
  288.2 51.0 %copy-start = (bf16[2,2,1,512,512]{4,3,2,1,0:T(8,128)(2,1)S(1)}, bf16[2,2,1,512,512]{4,3,2,1,0:T(8,128)(2,1)}, u32[]{:S(2)}) copy-start(bf16[2,2,1,512,512]{4,3,2,1,0:T(8,128)(2,1)} %param.14) | copy-start | bytes 6291460
  339.5 1.0 copy-start.4
  339.5 1.0 copy-start.6
Sparse Core Ops, SparseCore 0:
  169.2 27.2 all-gather.3
  198.3 89.8 all-gather.5
